TPU v7x, 256 devices: a whole 4x4x8 slice. The times are simulated.
256 devices in a mesh: task: 8 (over x, core), fsdp: 32 (over z, y).
Axes of the slice: x: 4, y: 4, z: 8, core: 2. Of those that a mesh axis runs over, the one named last changes fastest.
Arguments:
- grads_first: bfloat16 [16, 4096, 4096], P('task', 'fsdp'), may hold values from -120 to 120
- weights_first: float32 [4096, 4096], P('fsdp', 'task'), may hold values from -6 to 6
- moment_first: float32 [4096, 4096], P('fsdp', 'task'), may hold values from -3 to 3
- variance_first: float32 [4096, 4096], P('fsdp', 'task'), may hold values from 0.0025 to 1
- grads_second: bfloat16 [16, 4096, 4096], P('task', 'fsdp'), may hold values from -120 to 120
- weights_second: float32 [4096, 4096], P('fsdp', 'task'), may hold values from -6 to 6
- moment_second: float32 [4096, 4096], P('fsdp', 'task'), may hold values from -3 to 3
- variance_second: float32 [4096, 4096], P('fsdp', 'task'), may hold values from 0.0025 to 1
Outputs:
- combined_first: float32 [4096, 4096], P('fsdp', 'task')
- new_weights_first: float32 [4096, 4096], P('fsdp', 'task')
- new_moment_first: float32 [4096, 4096], P('fsdp', 'task')
- new_variance_first: float32 [4096, 4096], P('fsdp', 'task')
- combined_second: float32 [4096, 4096], P('fsdp', 'task')
- new_weights_second: float32 [4096, 4096], P('fsdp', 'task')
- new_moment_second: float32 [4096, 4096], P('fsdp', 'task')
- new_variance_second: float32 [4096, 4096], P('fsdp', 'task')
All inputs are finite; a program needn't handle non-finite values.
Results may differ from a plain program's by a relative error of at most 0.0006.
Values may be sent and summed in bfloat16 or wider, within the bound.
A program may use at most 128 MiB of HBM per device.

v0:
```python
import jax
import jax.numpy as jnp
from jax import lax
from jax.sharding import PartitionSpec as P

ITERS = 20


temper = 0.05
beta_one = 0.9
beta_two = 0.999
learn_rate = 0.001
adam_step = 1000.0
epsilon = 1e-08


def frank_wolfe(gram):
    scaled = gram / jnp.max(jnp.diagonal(gram))

    def advance(iteration, mixture):
        slope = 2.0 * jnp.dot(scaled, mixture, precision=lax.Precision.HIGHEST)
        expweights = jnp.exp(-slope / temper)
        vertex = expweights / jnp.sum(expweights)
        stepsize = 2.0 / (jnp.asarray(iteration).astype(jnp.float32) + 2.0)
        return mixture + stepsize * (vertex - mixture)

    start_mix = jnp.full((gram.shape[0],), 1.0 / gram.shape[0], jnp.float32)
    return lax.fori_loop(0, ITERS, advance, start_mix)


def adam_update(weights, moment, variance, combined):
    new_moment = beta_one * moment + (1.0 - beta_one) * combined
    new_variance = beta_two * variance + (1.0 - beta_two) * combined * combined
    corrected = new_moment / (1.0 - beta_one**adam_step)
    scaled_var = new_variance / (1.0 - beta_two**adam_step)
    new_weights = weights - learn_rate * corrected / (jnp.sqrt(scaled_var) + epsilon)
    return (new_weights, new_moment, new_variance)


def weighted_sum(mixture, stacked):
    return jnp.sum(mixture[:, None, None] * stacked.astype(jnp.float32), axis=0)


def prepare_first(gradients):
    regrouped = lax.all_to_all(gradients, "task", split_axis=2, concat_axis=0, tiled=True)
    return (
        regrouped,
        jnp.einsum("tre,sre->ts", regrouped, regrouped, preferred_element_type=jnp.float32),
    )


def prepare_second(gradients):
    regrouped = lax.all_to_all(gradients, "task", split_axis=2, concat_axis=0, tiled=True)
    return (
        regrouped,
        jnp.einsum("tre,sre->ts", regrouped, regrouped, preferred_element_type=jnp.float32),
    )


def combine_first(retained, mixture):
    return weighted_sum(mixture, retained)


def combine_second(retained, mixture):
    return weighted_sum(mixture, retained)


def local(
    grads_first,
    weights_first,
    moment_first,
    variance_first,
    grads_second,
    weights_second,
    moment_second,
    variance_second,
):
    retained_first, partial_first = prepare_first(grads_first)
    retained_second, partial_second = prepare_second(grads_second)
    gram_first, gram_second = lax.psum((partial_first, partial_second), ("task", "fsdp"))
    mixture_first = frank_wolfe(gram_first)
    mixture_second = frank_wolfe(gram_second)
    combined_first = combine_first(retained_first, mixture_first)
    first_w, first_m, first_v = adam_update(
        weights_first, moment_first, variance_first, combined_first
    )
    combined_second = combine_second(retained_second, mixture_second)
    second_w, second_m, second_v = adam_update(
        weights_second, moment_second, variance_second, combined_second
    )
    return (
        combined_first,
        first_w,
        first_m,
        first_v,
        combined_second,
        second_w,
        second_m,
        second_v,
    )


def solution(mesh):
    in_specs = (
        P("task", "fsdp", None),
        P("fsdp", "task"),
        P("fsdp", "task"),
        P("fsdp", "task"),
        P("task", "fsdp", None),
        P("fsdp", "task"),
        P("fsdp", "task"),
        P("fsdp", "task"),
    )
    out_specs = (
        P("fsdp", "task"),
        P("fsdp", "task"),
        P("fsdp", "task"),
        P("fsdp", "task"),
        P("fsdp", "task"),
        P("fsdp", "task"),
        P("fsdp", "task"),
        P("fsdp", "task"),
    )
    return jax.shard_map(local, mesh=mesh, in_specs=in_specs, out_specs=out_specs, check_vma=False)
```

profile of v0, /device:TPU:1, one launch (start us, length us, event | category | flops | bytes accessed | tf_op | source)
XLA Modules:
  0.0 235.0 jit_solution(9579224308458622726)
XLA Ops:
  0.6 6.2 %copy.25 = bf16[2,128,4096]{1,0,2:T(2,128)(2,1)} copy(bf16[2,128,4096]{2,1,0:T(8,128)(2,1)} %param.16) | data formatting | bytes 4194304 | tf_op args[4]
  6.8 6.7 %all-to-all-start.1 = ((bf16[2,128,4096]{1,0,2:T(2,128)(2,1)}), bf16[2,128,4096]{1,0,2:T(2,128)(2,1)S(1)}, u32[]{:S(2)}, u32[]{:S(2)}) async-start(bf16[2,128,4096]{1,0,2:T(2,128)(2,1)} %copy.25), calls=%async_computation.1 | async-start | bytes 4194304 | tf_op jit(solution)/shard_map/all_to_all | solution.py:53
  13.6 6.2 %copy.20 = bf16[2,128,4096]{1,0,2:T(2,128)(2,1)} copy(bf16[2,128,4096]{2,1,0:T(8,128)(2,1)} %param.12) | data formatting | bytes 4194304 | tf_op args[0]
  19.7 20.2 %all-to-all-done.1 = bf16[2,128,4096]{1,0,2:T(2,128)(2,1)S(1)} async-done(((bf16[2,128,4096]{1,0,2:T(2,128)(2,1)}), bf16[2,128,4096]{1,0,2:T(2,128)(2,1)S(1)}, u32[]{:S(2)}, u32[]{:S(2)}) %all-to-all-start.1) | async-done | bytes 2097184 | tf_op jit(solution)/shard_map/all_to_all | solution.py:53
  39.9 1.3 copy-done
  41.2 4.4 %all-to-all-start = ((bf16[2,128,4096]{1,0,2:T(2,128)(2,1)}), bf16[2,128,4096]{1,0,2:T(2,128)(2,1)S(1)}, u32[]{:S(2)}, u32[]{:S(2)}) async-start(bf16[2,128,4096]{1,0,2:T(2,128)(2,1)} %copy.20), calls=%async_computation | async-start | bytes 4194304 | tf_op jit(solution)/shard_map/all_to_all | solution.py:45
  45.8 0.8 copy.28
  46.6 0.8 copy.29
  47.6 1.1 copy.23
  48.8 3.0 %copy.26 = bf16[2,128,8,512]{1,0,2,3:T(2,128)(2,1)S(1)} copy(bf16[2,128,8,512]{1,0,3,2:T(2,128)(2,1)} %bitcast.62) | data formatting | bytes 4194304 | tf_op jit(solution)/shard_map/all_to_all | solution.py:53
  51.8 0.9 convolution_bitcast_fusion.2
  52.7 19.2 %all-to-all-done = bf16[2,128,4096]{1,0,2:T(2,128)(2,1)S(1)} async-done(((bf16[2,128,4096]{1,0,2:T(2,128)(2,1)}), bf16[2,128,4096]{1,0,2:T(2,128)(2,1)S(1)}, u32[]{:S(2)}, u32[]{:S(2)}) %all-to-all-start) | async-done | bytes 2097184 | tf_op jit(solution)/shard_map/all_to_all | solution.py:45
  72.0 1.4 copy.21
  73.4 0.9 convolution_bitcast_fusion.3
  74.3 78.4 %all-reduce = (f32[16,16]{1,0:T(8,128)S(1)}, f32[16,16]{1,0:T(8,128)S(1)}) all-reduce(f32[16,16]{1,0:T(8,128)S(1)} %convolution_bitcast_fusion.3, f32[16,16]{1,0:T(8,128)S(1)} %convolution_bitcast_fusion.2), channel_id=1, replica_groups=mesh['task'=8,'fsdp'=32] {'task','fsdp'}, use_global_device_ids=true, to_apply=%region_0.0 | all-reduce | flops 512 | bytes 4096 | tf_op jit(solution)/shard_map/psum | solution.py:80
  155.2 1.3 broadcast_divide_fusion
  156.5 29.4 %while.29 = (s32[]{:T(128)}, f32[16]{0:T(128)S(1)}, f32[16,16]{1,0:T(8,128)S(1)}, s32[]{:T(128)}, s32[]{:T(128)}, /*index=5*/f32[]{:T(128)}) while((s32[]{:T(128)}, f32[16]{0:T(128)S(1)}, f32[16,16]{1,0:T(8,128)S(1)}, s32[]{:T(128)}, s32[]{:T(128)}, /*index=5*/f32[]{:T(128)}) %tuple.78), condition=%wide.region_10.11_spmd.clone, body=%wide.region_8.10_spmd.clone.sunk | while | flops 3237 | bytes 1468 | solution.py:28
  156.6 0.7 fusion.31
  158.0 0.7 fusion.31
  159.5 0.7 fusion.31
  162.4 0.7 fusion.31
  163.9 0.7 fusion.31
  165.4 0.7 fusion.31
  168.3 0.7 fusion.31
  169.8 0.7 fusion.31
  171.3 0.7 fusion.31
  174.2 0.7 fusion.31
  175.7 0.7 fusion.31
  177.2 0.7 fusion.31
  178.6 0.7 fusion.31
  180.1 0.7 fusion.31
  181.6 0.7 fusion.31
  183.1 0.7 fusion.31
  184.5 0.7 fusion.31
  186.1 4.7 %multiply_reduce_fusion = f32[128,512]{0,1:T(8,128)S(1)} fusion(f32[8,2]{1,0:T(8,128)S(1)} %mul.109, bf16[2,128,8,512]{1,0,3,2:T(2,128)(2,1)} %bitcast.63), kind=kLoop, calls=%fused_computation.22 | loop fusion | flops 3080192 | bytes 2359360 | tf_op jit(solution)/shard_map/reduce_sum | solution.py:41
  190.7 0.8 copy.34
  191.6 2.0 divide_subtract_fusion.2
  193.6 1.8 copy.35
  195.4 1.8 copy.36
  197.1 1.8 copy.37
  198.9 29.4 %while.28 = (s32[]{:T(128)}, f32[16]{0:T(128)S(1)}, f32[16,16]{1,0:T(8,128)S(1)}, s32[]{:T(128)}, s32[]{:T(128)}, /*index=5*/f32[]{:T(128)}) while((s32[]{:T(128)}, f32[16]{0:T(128)S(1)}, f32[16,16]{1,0:T(8,128)S(1)}, s32[]{:T(128)}, s32[]{:T(128)}, /*index=5*/f32[]{:T(128)}) %tuple.75), condition=%wide.region_4.0_spmd.clone, body=%wide.region_2.0_spmd.clone.sunk | while | flops 3237 | bytes 1468 | solution.py:28
  200.4 0.7 fusion.29
  201.9 0.7 fusion.29
  228.4 3.1 %multiply_reduce_fusion.1 = f32[128,512]{0,1:T(8,128)S(1)} fusion(f32[8,2]{1,0:T(8,128)S(1)} %mul.100, bf16[2,128,8,512]{1,0,3,2:T(2,128)(2,1)S(1)} %bitcast.61), kind=kLoop, calls=%fused_computation.23 | loop fusion | flops 3080192 | bytes 2359360 | tf_op jit(solution)/shard_map/reduce_sum | solution.py:41
  231.5 0.8 copy.30
  232.5 0.8 copy.31
  233.4 0.8 copy.32
  234.2 0.8 copy.33
  (85 shorter events, 45.4 us)
Async XLA Ops:
  6.8 33.1 %all-to-all-start.1 = ((bf16[2,128,4096]{1,0,2:T(2,128)(2,1)}), bf16[2,128,4096]{1,0,2:T(2,128)(2,1)S(1)}, u32[]{:S(2)}, u32[]{:S(2)}) async-start(bf16[2,128,4096]{1,0,2:T(2,128)(2,1)} %copy.25), calls=%async_computation.1 | async-start | bytes 4194304 | tf_op jit(solution)/shard_map/all_to_all | solution.py:53
  19.7 25.9 %copy-start.1 = (f32[128,512]{1,0:T(8,128)S(1)}, f32[128,512]{1,0:T(8,128)}, u32[]{:S(2)}) copy-start(f32[128,512]{1,0:T(8,128)} %param.18) | copy-start | bytes 786436
  19.7 26.0 %copy-start.2 = (f32[128,512]{1,0:T(8,128)S(1)}, f32[128,512]{1,0:T(8,128)}, u32[]{:S(2)}) copy-start(f32[128,512]{1,0:T(8,128)} %param.19) | copy-start | bytes 786436
  19.7 26.9 %copy-start.3 = (f32[128,512]{1,0:T(8,128)S(1)}, f32[128,512]{1,0:T(8,128)}, u32[]{:S(2)}) copy-start(f32[128,512]{1,0:T(8,128)} %param.17) | copy-start | bytes 786436
  19.7 27.7 %copy-start.4 = (f32[128,512]{1,0:T(8,128)S(1)}, f32[128,512]{1,0:T(8,128)}, u32[]{:S(2)}) copy-start(f32[128,512]{1,0:T(8,128)} %param.14) | copy-start | bytes 786436
  39.9 1.3 copy-start
  41.2 30.7 %all-to-all-start = ((bf16[2,128,4096]{1,0,2:T(2,128)(2,1)}), bf16[2,128,4096]{1,0,2:T(2,128)(2,1)S(1)}, u32[]{:S(2)}, u32[]{:S(2)}) async-start(bf16[2,128,4096]{1,0,2:T(2,128)(2,1)} %copy.20), calls=%async_computation | async-start | bytes 4194304 | tf_op jit(solution)/shard_map/all_to_all | solution.py:45
  45.7 2.9 %copy-start.5 = (f32[128,512]{1,0:T(8,128)S(1)}, f32[128,512]{1,0:T(8,128)}, u32[]{:S(2)}) copy-start(f32[128,512]{1,0:T(8,128)} %param.13) | copy-start | bytes 786436
where the time goes:
time: 236 us; the launch traced here: 235 us
  blocking collectives  78.4 us (33%)
  waiting for transfers between devices  39.4 us (17%)
  other arithmetic  38.9 us (16%)
  local copies, waits for them, and re-layouts  32.3 us (14%)
  matrix products  31.6 us (13%)
  starting transfers between devices  11.1 us (5%)
  loops' own time  2.61 us (1%)
    psum x1, blocking collectives, local(): lax.psum((partial_first, partial_second), ('task', 'fsdp'))  78.4 us
    dot_general x40, matrix products, advance(): slope = 2.0 * jnp.dot(scaled, mixture, precision=lax.Precision.HIGHEST)  29.8 us
    add x40, other arithmetic, advance(): return mixture + stepsize * (vertex - mixture)  26.5 us
    unnamed x28, local copies, waits for them, and re-layouts  26.3 us
    all_to_all x1, waiting for transfers between devices, prepare_second(): lax.all_to_all(gradients, 'task', split_axis=2, concat_axis=0, tiled=True)  20.2 us
    all_to_all x1, waiting for transfers between devices, prepare_first(): lax.all_to_all(gradients, 'task', split_axis=2, concat_axis=0, tiled=True)  19.2 us
    reduce_sum x2, other arithmetic, weighted_sum(): return jnp.sum(mixture[:, None, None] * stacked.astype(jnp.float32), axis=0)  7.72 us
    all_to_all x1, starting transfers between devices, prepare_second(): lax.all_to_all(gradients, 'task', split_axis=2, concat_axis=0, tiled=True)  6.74 us
  transfers between devices with their start and end apart: 2, of which 2 were waited for; matrix products, arithmetic and copies ran while one was open for 6% of the time, Pallas kernels for 0%

commit v1 on v0

v1 whole, which is shorter than its diff:
```python
import functools

import jax
import jax.numpy as jnp
from jax import lax
from jax.experimental import pallas as pl
from jax.experimental.pallas import tpu as pltpu
from jax.sharding import PartitionSpec as P

ITERS = 20

temper = 0.05
beta_one = 0.9
beta_two = 0.999
learn_rate = 0.001
adam_step = 1000.0
epsilon = 1e-08

MESH = pl.DeviceIdType.MESH
TASKS = 16
CORES = 2
CHIPS_X = 4
CHIPS_Y = 4
CHIPS_Z = 8
LANES = 128
ROW_BLOCK = 16
PIECES = ((0, 0, 128), (1, 0, 64), (1, 64, 64))


def gram_block(received, first_row, rows):
    sides = [
        received[:, row : row + ROW_BLOCK, :].reshape(TASKS * ROW_BLOCK, received.shape[2])
        for row in range(first_row, first_row + rows, ROW_BLOCK)
    ]
    side = jnp.concatenate(sides, axis=1)
    return lax.dot_general(
        side, side, (((1,), (1,)), ((), ())), preferred_element_type=jnp.float32
    )


def fold_gram(blocks):
    size = TASKS * ROW_BLOCK
    row = lax.broadcasted_iota(jnp.int32, (size, size), 0)
    column = lax.broadcasted_iota(jnp.int32, (size, size), 1)
    same = (row % ROW_BLOCK) == (column % ROW_BLOCK)
    task_of = lax.broadcasted_iota(jnp.int32, (size, LANES), 0) // ROW_BLOCK
    lane = lax.broadcasted_iota(jnp.int32, (size, LANES), 1)
    gram = None
    for group, block in enumerate(blocks):
        kept = jnp.where(same, block, 0.0)
        rows_done = jnp.sum(kept.reshape(TASKS, ROW_BLOCK, size), axis=1)
        place = jnp.where(lane == task_of + group * TASKS, 1.0, 0.0)
        part = jnp.dot(
            rows_done, place, precision=lax.Precision.HIGHEST, preferred_element_type=jnp.float32
        )
        gram = part if gram is None else gram + part
    return gram[0:8] + pltpu.roll(gram[8:16], 2 * TASKS, 1)


def exchange_kernel(
    first_ref,
    second_ref,
    first_out,
    second_out,
    gram_out,
    parts,
    slots_y,
    slots_z,
    slots_x,
    piece_send,
    piece_recv,
    stage_send,
    stage_recv,
):
    task = lax.axis_index("task")
    fsdp = lax.axis_index("fsdp")
    chip_x, core = task // CORES, task % CORES
    chip_z, chip_y = fsdp // CHIPS_Y, fsdp % CHIPS_Y
    peers_x = [(lax.rem(task + k, CORES * CHIPS_X), fsdp) for k in range(1, CORES * CHIPS_X)]
    peers_y = [(task, chip_z * CHIPS_Y + lax.rem(chip_y + k, CHIPS_Y)) for k in range(1, CHIPS_Y)]
    peers_z = [(task, lax.rem(chip_z + k, CHIPS_Z) * CHIPS_Y + chip_y) for k in range(1, CHIPS_Z)]

    barrier = pltpu.get_barrier_semaphore()
    everyone = peers_x + peers_y + peers_z
    for peer in everyone:
        pl.semaphore_signal(barrier, inc=1, device_id=peer, device_id_type=MESH)
    pl.semaphore_wait(barrier, len(everyone))

    sources = (first_ref, second_ref)
    received = (first_out, second_out)
    width = first_out.shape[2]
    held = first_ref.shape[0]

    order = []
    for step in (2, 1, 3):
        for other in range(CORES):
            order.append(lax.rem(chip_x + step, CHIPS_X) * CORES + lax.rem(core + other, CORES))
    order.append(chip_x * CORES + (1 - core))

    for index, (group, row, rows) in enumerate(PIECES):
        landing = received[group].at[pl.ds(task * held, held), pl.ds(row, rows), :]
        for target in order:
            columns = pl.ds(pl.multiple_of(target * width, width), width)
            pltpu.make_async_remote_copy(
                src_ref=sources[group].at[:, pl.ds(row, rows), columns],
                dst_ref=landing,
                send_sem=piece_send.at[index],
                recv_sem=piece_recv.at[index],
                device_id=(target, fsdp),
                device_id_type=MESH,
            ).start()
        columns = pl.ds(pl.multiple_of(task * width, width), width)
        pltpu.make_async_copy(
            sources[group].at[:, pl.ds(row, rows), columns], landing, piece_recv.at[index]
        ).start()

    blocks = [None, None]
    for index, (group, row, rows) in enumerate(PIECES):
        whole = received[group].at[:, pl.ds(row, rows), :]
        pltpu.make_async_copy(whole, whole, piece_recv.at[index]).wait()
        block = gram_block(received[group], row, rows)
        blocks[group] = block if blocks[group] is None else blocks[group] + block
    total = fold_gram(blocks)

    stages = (
        (peers_y, chip_y, slots_y),
        (peers_z, chip_z, slots_z),
        (peers_x, task, slots_x),
    )
    for stage, (peers, mine, slots) in enumerate(stages):
        parts[stage] = total
        for peer in peers:
            pltpu.make_async_remote_copy(
                src_ref=parts.at[stage],
                dst_ref=slots.at[mine],
                send_sem=stage_send.at[stage],
                recv_sem=stage_recv.at[stage],
                device_id=peer,
                device_id_type=MESH,
            ).start()
        slots[mine] = total
        arrived = slots.at[pl.ds(0, len(peers))]
        pltpu.make_async_copy(arrived, arrived, stage_recv.at[stage]).wait()
        total = slots[0]
        for member in range(1, len(peers) + 1):
            total = total + slots[member]
    gram_out[...] = total

    for index, (group, row, rows) in enumerate(PIECES):
        sent = received[group].at[pl.ds(0, len(order) * held), pl.ds(row, rows), :]
        pltpu.make_async_copy(sent, sent, piece_send.at[index]).wait()
    for stage, (peers, mine, slots) in enumerate(stages):
        sent = slots.at[pl.ds(0, len(peers))]
        pltpu.make_async_copy(sent, sent, stage_send.at[stage]).wait()


def frank_wolfe(gram):
    lane = lax.broadcasted_iota(jnp.int32, (8, LANES), 1)
    is_first = lane < LANES // 2

    def spread(at):
        return jnp.broadcast_to(gram[:, at : at + 1], (8, LANES))

    columns = []
    for task in range(TASKS):
        upper = jnp.where(is_first, spread(task), spread(TASKS + task))
        lower = jnp.where(is_first, spread(2 * TASKS + task), spread(3 * TASKS + task))
        columns.append((upper, lower))

    def row_of(pair, task):
        return jnp.broadcast_to(pair[task // 8][task % 8 : task % 8 + 1, :], (8, LANES))

    def tree(terms, combine):
        while len(terms) > 1:
            paired = [combine(terms[i], terms[i + 1]) for i in range(0, len(terms) - 1, 2)]
            terms = paired + terms[len(paired) * 2 :]
        return terms[0]

    largest = tree([row_of(columns[task], task) for task in range(TASKS)], jnp.maximum)
    steep = [tuple((part / largest) * (-2.0 / temper) for part in pair) for pair in columns]

    start = jnp.full((8, LANES), 1.0 / TASKS, jnp.float32)
    slope = [tree([steep[task][half] * (1.0 / TASKS) for task in range(TASKS)], jnp.add) for half in range(2)]
    mixture = [start, start]
    for iteration in range(ITERS):
        step = 2.0 / (iteration + 2.0)
        weight = [jnp.exp(half) for half in slope]
        rows = [row_of(weight, task) for task in range(TASKS)]
        scale = step / tree(rows, jnp.add)
        moved = [tree([steep[task][half] * rows[task] for task in range(TASKS)], jnp.add) for half in range(2)]
        slope = [(1.0 - step) * slope[half] + scale * moved[half] for half in range(2)]
        mixture = [(1.0 - step) * mixture[half] + scale * weight[half] for half in range(2)]
    return mixture


UPDATE_ROWS = 32


def update_kernel(
    gram_ref,
    first_ref,
    second_ref,
    first_w,
    first_m,
    first_v,
    second_w,
    second_m,
    second_v,
    out_first_c,
    out_first_w,
    out_first_m,
    out_first_v,
    out_second_c,
    out_second_w,
    out_second_m,
    out_second_v,
    state,
    result,
    mixes,
    in_sem,
    out_sem,
):
    stored = ((first_w, first_m, first_v), (second_w, second_m, second_v))
    outputs = (
        (out_first_c, out_first_w, out_first_m, out_first_v),
        (out_second_c, out_second_w, out_second_m, out_second_v),
    )
    loads = []
    for group in range(2):
        for kind in range(3):
            copy = pltpu.make_async_copy(
                stored[group][kind], state.at[group, kind], in_sem.at[group, kind]
            )
            copy.start()
            loads.append(copy)

    mixture = frank_wolfe(gram_ref[...])
    for half in range(2):
        mixes[8 * half : 8 * half + 8, :] = mixture[half]

    for copy in loads:
        copy.wait()

    rows_all, width = state.shape[2], state.shape[3]
    retained = (first_ref, second_ref)
    stores = []
    for group in range(2):
        lanes = slice(group * (LANES // 2), group * (LANES // 2) + 1)
        weights_of = [
            jnp.broadcast_to(mixes[task : task + 1, lanes], (1, width)) for task in range(TASKS)
        ]
        for block in range(rows_all // UPDATE_ROWS):
            rows = slice(block * UPDATE_ROWS, (block + 1) * UPDATE_ROWS)
            combined = None
            for task in range(TASKS):
                term = weights_of[task] * retained[group][task, rows, :].astype(jnp.float32)
                combined = term if combined is None else combined + term
            weights = state[group, 0, rows, :]
            moment = state[group, 1, rows, :]
            variance = state[group, 2, rows, :]
            new_moment = beta_one * moment + (1.0 - beta_one) * combined
            new_variance = beta_two * variance + (1.0 - beta_two) * combined * combined
            corrected = new_moment / (1.0 - beta_one**adam_step)
            scaled_var = new_variance / (1.0 - beta_two**adam_step)
            new_weights = weights - learn_rate * corrected / (jnp.sqrt(scaled_var) + epsilon)
            values = (combined, new_weights, new_moment, new_variance)
            for kind, value in enumerate(values):
                result[group, kind, rows, :] = value
                copy = pltpu.make_async_copy(
                    result.at[group, kind, rows, :],
                    outputs[group][kind].at[rows, :],
                    out_sem.at[group, block, kind],
                )
                copy.start()
                stores.append(copy)
    for copy in stores:
        copy.wait()


def local(
    grads_first,
    weights_first,
    moment_first,
    variance_first,
    grads_second,
    weights_second,
    moment_second,
    variance_second,
):
    held, rows, columns = grads_first.shape
    width = weights_first.shape[1]
    any_space = pl.BlockSpec(memory_space=pl.ANY)
    in_vmem = pl.BlockSpec(memory_space=pltpu.VMEM)
    in_hbm = pl.BlockSpec(memory_space=pltpu.HBM)
    tile = (8, LANES)
    first, second, gram = pl.pallas_call(
        exchange_kernel,
        name="exchange",
        out_shape=(
            pltpu.VMEM((TASKS, rows, width), jnp.bfloat16),
            pltpu.VMEM((TASKS, rows, width), jnp.bfloat16),
            pltpu.VMEM(tile, jnp.float32),
        ),
        in_specs=[in_hbm, in_hbm],
        out_specs=(in_vmem, in_vmem, in_vmem),
        scratch_shapes=[
            pltpu.VMEM((3,) + tile, jnp.float32),
            pltpu.VMEM((CHIPS_Y,) + tile, jnp.float32),
            pltpu.VMEM((CHIPS_Z,) + tile, jnp.float32),
            pltpu.VMEM((CORES * CHIPS_X,) + tile, jnp.float32),
            pltpu.SemaphoreType.DMA((len(PIECES),)),
            pltpu.SemaphoreType.DMA((len(PIECES),)),
            pltpu.SemaphoreType.DMA((3,)),
            pltpu.SemaphoreType.DMA((3,)),
        ],
        compiler_params=pltpu.CompilerParams(
            collective_id=0, has_side_effects=True, vmem_limit_bytes=32 * 1024 * 1024
        ),
    )(grads_first, grads_second)

    shape = jax.ShapeDtypeStruct((rows, width), jnp.float32)
    return pl.pallas_call(
        update_kernel,
        name="update",
        out_shape=(shape,) * 8,
        in_specs=[in_vmem] * 3 + [any_space] * 6,
        out_specs=(in_hbm,) * 8,
        scratch_shapes=[
            pltpu.VMEM((2, 3, rows, width), jnp.float32),
            pltpu.VMEM((2, 4, rows, width), jnp.float32),
            pltpu.VMEM((TASKS, LANES), jnp.float32),
            pltpu.SemaphoreType.DMA((2, 3)),
            pltpu.SemaphoreType.DMA((2, rows // UPDATE_ROWS, 4)),
        ],
        compiler_params=pltpu.CompilerParams(vmem_limit_bytes=32 * 1024 * 1024),
    )(
        gram,
        first,
        second,
        weights_first,
        moment_first,
        variance_first,
        weights_second,
        moment_second,
        variance_second,
    )


def solution(mesh):
    in_specs = (
        P("task", "fsdp", None),
        P("fsdp", "task"),
        P("fsdp", "task"),
        P("fsdp", "task"),
        P("task", "fsdp", None),
        P("fsdp", "task"),
        P("fsdp", "task"),
        P("fsdp", "task"),
    )
    out_specs = (P("fsdp", "task"),) * 8
    return jax.shard_map(local, mesh=mesh, in_specs=in_specs, out_specs=out_specs, check_vma=False)
```

time: 236 us -> 77.8 us (0.33)
  blocking collectives: 78.4 us -> 0 us
  Pallas kernels: 0 us -> 73.7 us
  waiting for transfers between devices: 39.4 us -> 0 us
  other arithmetic: 38.9 us -> 0 us
  matrix products: 31.6 us -> 0 us
  local copies, waits for them, and re-layouts: 32.3 us -> 3.2 us
  starting transfers between devices: 11.1 us -> 0 us
  loops' own time: 2.61 us -> 0 us
    psum x1 -> x0, blocking collectives: 78.4 us -> none  [local(): lax.psum((partial_first, partial_second), ('task', 'fsdp'))]
    pallas_call x0 -> x2, Pallas kernels: none -> 73.7 us  [the longest x1 70.6 us: local(): pl.pallas_call(exchange_kernel, name='exchange', out_shape=(pltpu.VMEM((T...]
    all_to_all x2 -> x0, waiting for transfers between devices: 39.4 us -> none  [the longest x1 20.2 us: prepare_second(): lax.all_to_all(gradients, 'task', split_axis=2, concat_axis=0, tiled=True)]
    dot_general x42 -> x0, matrix products: 31.6 us -> none  [the longest x40 29.8 us: advance(): slope = 2.0 * jnp.dot(scaled, mixture, precision=lax.Precision.HIGHEST)]
    add x40 -> x0, other arithmetic: 26.5 us -> none  [advance(): return mixture + stepsize * (vertex - mixture)]
    unnamed x28 -> x16, local copies, waits for them, and re-layouts: 26.3 us -> 3.2 us
    all_to_all x2 -> x0, starting transfers between devices: 11.1 us -> none  [the longest x1 6.74 us: prepare_second(): lax.all_to_all(gradients, 'task', split_axis=2, concat_axis=0, tiled=True)]
    reduce_sum x2 -> x0, other arithmetic: 7.72 us -> none  [weighted_sum(): return jnp.sum(mixture[:, None, None] * stacked.astype(jnp.float32), axis=0)]
  transfers between devices with their start and end apart: 2 -> 0, of which waited for: 2 -> 0; matrix products, arithmetic and copies ran while one was open for 6% -> 0% of each run, Pallas kernels for 0% -> 0%
where the time goes in v1:
time: 77.8 us; the launch traced here: 77.6 us
  Pallas kernels  73.7 us (95%)
  local copies, waits for them, and re-layouts  3.2 us (4%)
    pallas_call x1, Pallas kernels, local(): pl.pallas_call(exchange_kernel, name='exchange', out_shape=(pltpu.VMEM((T...  70.6 us
    unnamed x16, local copies, waits for them, and re-layouts  3.2 us
    pallas_call x1, Pallas kernels, local(): pl.pallas_call(update_kernel, name='update', out_shape=(shape,) * 8, in_s...  3.16 us

profile of v1, /device:TPU:1, one launch (start us, length us, event | category | flops | bytes accessed | tf_op | source)
XLA Modules:
  0.0 77.6 jit_solution(15691986099797274822)
XLA Ops:
  0.6 0.0 copy-start
  0.6 1.6 %copy-done = bf16[2,128,4096]{2,1,0:T(8,128)(2,1)S(1)} copy-done((bf16[2,128,4096]{2,1,0:T(8,128)(2,1)S(1)}, bf16[2,128,4096]{2,1,0:T(8,128)(2,1)}, u32[]{:S(2)}) %copy-start) | copy-done | bytes 2097176
  2.2 0.0 copy-start.1
  2.2 1.6 %copy-done.1 = bf16[2,128,4096]{2,1,0:T(8,128)(2,1)S(1)} copy-done((bf16[2,128,4096]{2,1,0:T(8,128)(2,1)S(1)}, bf16[2,128,4096]{2,1,0:T(8,128)(2,1)}, u32[]{:S(2)}) %copy-start.1) | copy-done | bytes 2097176
  3.8 0.0 copy-start.2
  3.8 0.0 copy-start.3
  3.8 0.0 copy-start.4
  3.8 0.0 copy-start.5
  3.8 0.0 copy-start.6
  3.8 0.0 copy-start.7
  3.9 70.6 %exchange.1 = (bf16[16,128,512]{2,1,0:T(8,128)(2,1)S(1)}, bf16[16,128,512]{2,1,0:T(8,128)(2,1)S(1)}, f32[8,128]{1,0:T(8,128)S(1)}) custom-call(bf16[2,128,4096]{2,1,0:T(8,128)(2,1)S(1)} %copy-done, bf16[2,128,4096]{2,1,0:T(8,128)(2,1)S(1)} %copy-done.1), custom_call_target="tpu_custom_call" | custom-call | tf_op jit(solution)/shard_map/exchange/pallas_call | solution.py:296
  74.4 0.0 copy-done.2
  74.4 0.0 copy-done.3
  74.4 0.0 copy-done.4
  74.4 0.0 copy-done.5
  74.5 0.0 copy-done.6
  74.5 0.0 copy-done.7
  74.5 3.2 %update.1 = (f32[128,512]{1,0:T(8,128)}, f32[128,512]{1,0:T(8,128)}, f32[128,512]{1,0:T(8,128)}, f32[128,512]{1,0:T(8,128)}, f32[128,512]{1,0:T(8,128)}, /*index...) custom-call(f32[8,128]{1,0:T(8,128)S(1)} %get-tuple-element.11.gram_ref, ...), custom_call_target="tpu_custom_call" | custom-call | tf_op jit(solution)/shard_map/update/pallas_call | solution.py:322
Async XLA Ops:
  0.6 1.6 %copy-start = (bf16[2,128,4096]{2,1,0:T(8,128)(2,1)S(1)}, bf16[2,128,4096]{2,1,0:T(8,128)(2,1)}, u32[]{:S(2)}) copy-start(bf16[2,128,4096]{2,1,0:T(8,128)(2,1)} %first_ref.1) | copy-start | bytes 6291460
  2.2 1.6 %copy-start.1 = (bf16[2,128,4096]{2,1,0:T(8,128)(2,1)S(1)}, bf16[2,128,4096]{2,1,0:T(8,128)(2,1)}, u32[]{:S(2)}) copy-start(bf16[2,128,4096]{2,1,0:T(8,128)(2,1)} %second_ref.1) | copy-start | bytes 6291460
  3.8 70.6 %copy-start.2 = (f32[128,512]{1,0:T(8,128)S(1)}, f32[128,512]{1,0:T(8,128)}, u32[]{:S(2)}) copy-start(f32[128,512]{1,0:T(8,128)} %first_w.1) | copy-start | bytes 786436
  3.8 70.6 %copy-start.3 = (f32[128,512]{1,0:T(8,128)S(1)}, f32[128,512]{1,0:T(8,128)}, u32[]{:S(2)}) copy-start(f32[128,512]{1,0:T(8,128)} %first_m.1) | copy-start | bytes 786436
  3.8 70.6 %copy-start.4 = (f32[128,512]{1,0:T(8,128)S(1)}, f32[128,512]{1,0:T(8,128)}, u32[]{:S(2)}) copy-start(f32[128,512]{1,0:T(8,128)} %first_v.1) | copy-start | bytes 786436
  3.8 70.6 %copy-start.5 = (f32[128,512]{1,0:T(8,128)S(1)}, f32[128,512]{1,0:T(8,128)}, u32[]{:S(2)}) copy-start(f32[128,512]{1,0:T(8,128)} %second_w.1) | copy-start | bytes 786436
  3.8 70.6 %copy-start.6 = (f32[128,512]{1,0:T(8,128)S(1)}, f32[128,512]{1,0:T(8,128)}, u32[]{:S(2)}) copy-start(f32[128,512]{1,0:T(8,128)} %second_m.1) | copy-start | bytes 786436
  3.8 70.6 %copy-start.7 = (f32[128,512]{1,0:T(8,128)S(1)}, f32[128,512]{1,0:T(8,128)}, u32[]{:S(2)}) copy-start(f32[128,512]{1,0:T(8,128)} %second_v.1) | copy-start | bytes 786436

commit v2 on v1

--- a/solution.py
+++ b/solution.py
@@ -24,7 +24,7 @@
 CHIPS_Z = 8
 LANES = 128
 ROW_BLOCK = 16
-PIECES = ((0, 0, 128), (1, 0, 64), (1, 64, 64))
+PIECES = ((0, 0, 128), (1, 0, 96), (1, 96, 32))
 
 
 def gram_block(received, first_row, rows):
@@ -54,7 +54,15 @@
             rows_done, place, precision=lax.Precision.HIGHEST, preferred_element_type=jnp.float32
         )
         gram = part if gram is None else gram + part
-    return gram[0:8] + pltpu.roll(gram[8:16], 2 * TASKS, 1)
+    half = gram[0:8] + pltpu.roll(gram[8:16], 2 * TASKS, 1)
+    return (half + pltpu.roll(pltpu.roll(half, LANES // 2, 1), 4, 0))[0:4]
+
+
+def tree(terms, combine):
+    while len(terms) > 1:
+        paired = [combine(terms[i], terms[i + 1]) for i in range(0, len(terms) - 1, 2)]
+        terms = paired + terms[len(paired) * 2 :]
+    return terms[0]
 
 
 def exchange_kernel(
@@ -64,13 +72,13 @@
     second_out,
     gram_out,
     parts,
-    slots_y,
+    slots_plane,
     slots_z,
-    slots_x,
     piece_send,
     piece_recv,
     stage_send,
     stage_recv,
+    entered,
 ):
     task = lax.axis_index("task")
     fsdp = lax.axis_index("fsdp")
@@ -80,11 +88,19 @@
     peers_y = [(task, chip_z * CHIPS_Y + lax.rem(chip_y + k, CHIPS_Y)) for k in range(1, CHIPS_Y)]
     peers_z = [(task, lax.rem(chip_z + k, CHIPS_Z) * CHIPS_Y + chip_y) for k in range(1, CHIPS_Z)]
 
+    peers_plane = [
+        (lax.rem(task + other, CORES * CHIPS_X), chip_z * CHIPS_Y + lax.rem(chip_y + step, CHIPS_Y))
+        for step in (2, 1, 3, 0)
+        for other in (4, 5, 3, 2, 6, 7, 1, 0)
+        if (step, other) != (0, 0)
+    ]
+    beside_z = [peers_z[0], peers_z[-1]]
+
     barrier = pltpu.get_barrier_semaphore()
-    everyone = peers_x + peers_y + peers_z
-    for peer in everyone:
+    near = peers_x + peers_y + beside_z
+    for peer in near:
         pl.semaphore_signal(barrier, inc=1, device_id=peer, device_id_type=MESH)
-    pl.semaphore_wait(barrier, len(everyone))
+    pl.semaphore_wait(barrier, len(near))
 
     sources = (first_ref, second_ref)
     received = (first_out, second_out)
@@ -114,6 +130,11 @@
             sources[group].at[:, pl.ds(row, rows), columns], landing, piece_recv.at[index]
         ).start()
 
+    for turn, tellers in enumerate((peers_y, beside_z, beside_z, beside_z)):
+        for peer in tellers:
+            pl.semaphore_signal(entered.at[turn], inc=1, device_id=peer, device_id_type=MESH)
+        pl.semaphore_wait(entered.at[turn], len(tellers))
+
     blocks = [None, None]
     for index, (group, row, rows) in enumerate(PIECES):
         whole = received[group].at[:, pl.ds(row, rows), :]
@@ -123,9 +144,8 @@
     total = fold_gram(blocks)
 
     stages = (
-        (peers_y, chip_y, slots_y),
+        (peers_plane, chip_y * CORES * CHIPS_X + task, slots_plane),
         (peers_z, chip_z, slots_z),
-        (peers_x, task, slots_x),
     )
     for stage, (peers, mine, slots) in enumerate(stages):
         parts[stage] = total
@@ -141,10 +161,9 @@
         slots[mine] = total
         arrived = slots.at[pl.ds(0, len(peers))]
         pltpu.make_async_copy(arrived, arrived, stage_recv.at[stage]).wait()
-        total = slots[0]
-        for member in range(1, len(peers) + 1):
-            total = total + slots[member]
-    gram_out[...] = total
+        total = tree([slots[member] for member in range(len(peers) + 1)], jnp.add)
+    gram_out[0:4, :] = total
+    gram_out[4:8, :] = pltpu.roll(total, LANES // 2, 1)
 
     for index, (group, row, rows) in enumerate(PIECES):
         sent = received[group].at[pl.ds(0, len(order) * held), pl.ds(row, rows), :]
@@ -169,12 +188,6 @@
 
     def row_of(pair, task):
         return jnp.broadcast_to(pair[task // 8][task % 8 : task % 8 + 1, :], (8, LANES))
-
-    def tree(terms, combine):
-        while len(terms) > 1:
-            paired = [combine(terms[i], terms[i + 1]) for i in range(0, len(terms) - 1, 2)]
-            terms = paired + terms[len(paired) * 2 :]
-        return terms[0]
 
     largest = tree([row_of(columns[task], task) for task in range(TASKS)], jnp.maximum)
     steep = [tuple((part / largest) * (-2.0 / temper) for part in pair) for pair in columns]
@@ -293,6 +306,7 @@
     in_vmem = pl.BlockSpec(memory_space=pltpu.VMEM)
     in_hbm = pl.BlockSpec(memory_space=pltpu.HBM)
     tile = (8, LANES)
+    packed = (4, LANES)
     first, second, gram = pl.pallas_call(
         exchange_kernel,
         name="exchange",
@@ -304,17 +318,17 @@
         in_specs=[in_hbm, in_hbm],
         out_specs=(in_vmem, in_vmem, in_vmem),
         scratch_shapes=[
-            pltpu.VMEM((3,) + tile, jnp.float32),
-            pltpu.VMEM((CHIPS_Y,) + tile, jnp.float32),
-            pltpu.VMEM((CHIPS_Z,) + tile, jnp.float32),
-            pltpu.VMEM((CORES * CHIPS_X,) + tile, jnp.float32),
+            pltpu.VMEM((2,) + packed, jnp.float32),
+            pltpu.VMEM((CHIPS_Y * CHIPS_X * CORES,) + packed, jnp.float32),
+            pltpu.VMEM((CHIPS_Z,) + packed, jnp.float32),
             pltpu.SemaphoreType.DMA((len(PIECES),)),
             pltpu.SemaphoreType.DMA((len(PIECES),)),
-            pltpu.SemaphoreType.DMA((3,)),
-            pltpu.SemaphoreType.DMA((3,)),
+            pltpu.SemaphoreType.DMA((2,)),
+            pltpu.SemaphoreType.DMA((2,)),
+            pltpu.SemaphoreType.REGULAR((4,)),
         ],
         compiler_params=pltpu.CompilerParams(
-            collective_id=0, has_side_effects=True, vmem_limit_bytes=32 * 1024 * 1024
+            collective_id=0, has_side_effects=True, vmem_limit_bytes=60 * 1000 * 1000
         ),
     )(grads_first, grads_second)
 

time: 77.8 us -> 71.5 us (0.919)
  local copies, waits for them, and re-layouts: 3.2 us -> 0.03 us
  Pallas kernels: 73.7 us -> 70.6 us
    unnamed x16 -> x12, local copies, waits for them, and re-layouts: 3.2 us -> 0.03 us
    pallas_call x1, Pallas kernels: 70.6 us -> 67.5 us  [local(): pl.pallas_call(exchange_kernel, name='exchange', out_shape=(pltpu.VMEM((T...]
where the time goes in v2:
time: 71.5 us; the launch traced here: 71.4 us
  Pallas kernels  70.6 us (99%)
  between operations  0.74 us (1%)
    pallas_call x1, Pallas kernels, local(): pl.pallas_call(exchange_kernel, name='exchange', out_shape=(pltpu.VMEM((T...  67.5 us
    pallas_call x1, Pallas kernels, local(): pl.pallas_call(update_kernel, name='update', out_shape=(shape,) * 8, in_s...  3.16 us

profile of v2, /device:TPU:1, one launch (start us, length us, event | category | flops | bytes accessed | tf_op | source)
XLA Modules:
  0.0 71.4 jit_solution(10768973936352296163)
XLA Ops:
  0.6 0.0 copy-start.5
  0.6 0.0 copy-start.4
  0.7 0.0 copy-start.3
  0.7 0.0 copy-start.2
  0.7 0.0 copy-start.1
  0.7 0.0 copy-start
  0.7 67.5 %exchange.1 = (bf16[16,128,512]{2,1,0:T(8,128)(2,1)S(1)}, bf16[16,128,512]{2,1,0:T(8,128)(2,1)S(1)}, f32[8,128]{1,0:T(8,128)S(1)}) custom-call(bf16[2,128,4096]{2,1,0:T(8,128)(2,1)} %first_ref.1, bf16[2,128,4096]{2,1,0:T(8,128)(2,1)} %second_ref.1), custom_call_target="tpu_custom_call" | custom-call | tf_op jit(solution)/shard_map/exchange/pallas_call | solution.py:310
  68.2 0.0 copy-done.5
  68.2 0.0 copy-done.4
  68.2 0.0 copy-done.3
  68.2 0.0 copy-done.2
  68.2 0.0 copy-done.1
  68.2 0.0 copy-done
  68.2 3.2 %update.1 = (f32[128,512]{1,0:T(8,128)}, f32[128,512]{1,0:T(8,128)}, f32[128,512]{1,0:T(8,128)}, f32[128,512]{1,0:T(8,128)}, f32[128,512]{1,0:T(8,128)}, /*index...) custom-call(f32[8,128]{1,0:T(8,128)S(1)} %get-tuple-element.11.gram_ref, ...), custom_call_target="tpu_custom_call" | custom-call | tf_op jit(solution)/shard_map/update/pallas_call | solution.py:336
Async XLA Ops:
  0.6 67.5 %copy-start.5 = (f32[128,512]{1,0:T(8,128)S(1)}, f32[128,512]{1,0:T(8,128)}, u32[]{:S(2)}) copy-start(f32[128,512]{1,0:T(8,128)} %second_v.1) | copy-start | bytes 786436
  0.6 67.5 %copy-start.4 = (f32[128,512]{1,0:T(8,128)S(1)}, f32[128,512]{1,0:T(8,128)}, u32[]{:S(2)}) copy-start(f32[128,512]{1,0:T(8,128)} %second_m.1) | copy-start | bytes 786436
  0.7 67.5 %copy-start.3 = (f32[128,512]{1,0:T(8,128)S(1)}, f32[128,512]{1,0:T(8,128)}, u32[]{:S(2)}) copy-start(f32[128,512]{1,0:T(8,128)} %second_w.1) | copy-start | bytes 786436
  0.7 67.5 %copy-start.2 = (f32[128,512]{1,0:T(8,128)S(1)}, f32[128,512]{1,0:T(8,128)}, u32[]{:S(2)}) copy-start(f32[128,512]{1,0:T(8,128)} %first_v.1) | copy-start | bytes 786436
  0.7 67.5 %copy-start.1 = (f32[128,512]{1,0:T(8,128)S(1)}, f32[128,512]{1,0:T(8,128)}, u32[]{:S(2)}) copy-start(f32[128,512]{1,0:T(8,128)} %first_m.1) | copy-start | bytes 786436
  0.7 67.5 %copy-start = (f32[128,512]{1,0:T(8,128)S(1)}, f32[128,512]{1,0:T(8,128)}, u32[]{:S(2)}) copy-start(f32[128,512]{1,0:T(8,128)} %first_w.1) | copy-start | bytes 786436

commit v3 on v2

--- a/solution.py
+++ b/solution.py
@@ -1,5 +1,3 @@
-import functools
-
 import jax
 import jax.numpy as jnp
 from jax import lax
@@ -24,7 +22,7 @@
 CHIPS_Z = 8
 LANES = 128
 ROW_BLOCK = 16
-PIECES = ((0, 0, 128), (1, 0, 96), (1, 96, 32))
+PIECES = ((0, 0, 128), (1, 0, 64), (1, 64, 48), (1, 112, 16))
 
 
 def gram_block(received, first_row, rows):
@@ -38,22 +36,19 @@
     )
 
 
-def fold_gram(blocks):
+def fold_gram(group, block):
     size = TASKS * ROW_BLOCK
     row = lax.broadcasted_iota(jnp.int32, (size, size), 0)
     column = lax.broadcasted_iota(jnp.int32, (size, size), 1)
     same = (row % ROW_BLOCK) == (column % ROW_BLOCK)
     task_of = lax.broadcasted_iota(jnp.int32, (size, LANES), 0) // ROW_BLOCK
     lane = lax.broadcasted_iota(jnp.int32, (size, LANES), 1)
-    gram = None
-    for group, block in enumerate(blocks):
-        kept = jnp.where(same, block, 0.0)
-        rows_done = jnp.sum(kept.reshape(TASKS, ROW_BLOCK, size), axis=1)
-        place = jnp.where(lane == task_of + group * TASKS, 1.0, 0.0)
-        part = jnp.dot(
-            rows_done, place, precision=lax.Precision.HIGHEST, preferred_element_type=jnp.float32
-        )
-        gram = part if gram is None else gram + part
+    kept = jnp.where(same, block, 0.0)
+    rows_done = jnp.sum(kept.reshape(TASKS, ROW_BLOCK, size), axis=1)
+    place = jnp.where(lane == task_of + group * TASKS, 1.0, 0.0)
+    gram = jnp.dot(
+        rows_done, place, precision=lax.Precision.HIGHEST, preferred_element_type=jnp.float32
+    )
     half = gram[0:8] + pltpu.roll(gram[8:16], 2 * TASKS, 1)
     return (half + pltpu.roll(pltpu.roll(half, LANES // 2, 1), 4, 0))[0:4]
 
@@ -135,13 +130,12 @@
             pl.semaphore_signal(entered.at[turn], inc=1, device_id=peer, device_id_type=MESH)
         pl.semaphore_wait(entered.at[turn], len(tellers))
 
-    blocks = [None, None]
+    total = None
     for index, (group, row, rows) in enumerate(PIECES):
         whole = received[group].at[:, pl.ds(row, rows), :]
         pltpu.make_async_copy(whole, whole, piece_recv.at[index]).wait()
-        block = gram_block(received[group], row, rows)
-        blocks[group] = block if blocks[group] is None else blocks[group] + block
-    total = fold_gram(blocks)
+        part = fold_gram(group, gram_block(received[group], row, rows))
+        total = part if total is None else total + part
 
     stages = (
         (peers_plane, chip_y * CORES * CHIPS_X + task, slots_plane),
@@ -227,10 +221,8 @@
     out_second_w,
     out_second_m,
     out_second_v,
-    state,
     result,
     mixes,
-    in_sem,
     out_sem,
 ):
     stored = ((first_w, first_m, first_v), (second_w, second_m, second_v))
@@ -238,23 +230,11 @@
         (out_first_c, out_first_w, out_first_m, out_first_v),
         (out_second_c, out_second_w, out_second_m, out_second_v),
     )
-    loads = []
-    for group in range(2):
-        for kind in range(3):
-            copy = pltpu.make_async_copy(
-                stored[group][kind], state.at[group, kind], in_sem.at[group, kind]
-            )
-            copy.start()
-            loads.append(copy)
-
     mixture = frank_wolfe(gram_ref[...])
     for half in range(2):
         mixes[8 * half : 8 * half + 8, :] = mixture[half]
 
-    for copy in loads:
-        copy.wait()
-
-    rows_all, width = state.shape[2], state.shape[3]
+    rows_all, width = first_w.shape
     retained = (first_ref, second_ref)
     stores = []
     for group in range(2):
@@ -268,14 +248,14 @@
             for task in range(TASKS):
                 term = weights_of[task] * retained[group][task, rows, :].astype(jnp.float32)
                 combined = term if combined is None else combined + term
-            weights = state[group, 0, rows, :]
-            moment = state[group, 1, rows, :]
-            variance = state[group, 2, rows, :]
+            weights = stored[group][0][rows, :]
+            moment = stored[group][1][rows, :]
+            variance = stored[group][2][rows, :]
             new_moment = beta_one * moment + (1.0 - beta_one) * combined
             new_variance = beta_two * variance + (1.0 - beta_two) * combined * combined
-            corrected = new_moment / (1.0 - beta_one**adam_step)
-            scaled_var = new_variance / (1.0 - beta_two**adam_step)
-            new_weights = weights - learn_rate * corrected / (jnp.sqrt(scaled_var) + epsilon)
+            moved = new_moment * (learn_rate / (1.0 - beta_one**adam_step))
+            scaled_var = new_variance * (1.0 / (1.0 - beta_two**adam_step))
+            new_weights = weights - moved / (jnp.sqrt(scaled_var) + epsilon)
             values = (combined, new_weights, new_moment, new_variance)
             for kind, value in enumerate(values):
                 result[group, kind, rows, :] = value
@@ -302,7 +282,6 @@
 ):
     held, rows, columns = grads_first.shape
     width = weights_first.shape[1]
-    any_space = pl.BlockSpec(memory_space=pl.ANY)
     in_vmem = pl.BlockSpec(memory_space=pltpu.VMEM)
     in_hbm = pl.BlockSpec(memory_space=pltpu.HBM)
     tile = (8, LANES)
@@ -337,13 +316,11 @@
         update_kernel,
         name="update",
         out_shape=(shape,) * 8,
-        in_specs=[in_vmem] * 3 + [any_space] * 6,
+        in_specs=[in_vmem] * 9,
         out_specs=(in_hbm,) * 8,
         scratch_shapes=[
-            pltpu.VMEM((2, 3, rows, width), jnp.float32),
             pltpu.VMEM((2, 4, rows, width), jnp.float32),
             pltpu.VMEM((TASKS, LANES), jnp.float32),
-            pltpu.SemaphoreType.DMA((2, 3)),
             pltpu.SemaphoreType.DMA((2, rows // UPDATE_ROWS, 4)),
         ],
         compiler_params=pltpu.CompilerParams(vmem_limit_bytes=32 * 1024 * 1024),

time: 71.5 us -> 70.3 us (0.983)
  Pallas kernels: 70.6 us -> 69.5 us
    pallas_call x1, Pallas kernels: 67.5 us -> 66.5 us  [local(): pl.pallas_call(exchange_kernel, name='exchange', out_shape=(pltpu.VMEM((T...]
where the time goes in v3:
time: 70.3 us
  Pallas kernels  69.5 us (99%)
  between operations  0.74 us (1%)
    pallas_call x1, Pallas kernels, local(): pl.pallas_call(exchange_kernel, name='exchange', out_shape=(pltpu.VMEM((T...  66.5 us
    pallas_call x1, Pallas kernels, local(): pl.pallas_call(update_kernel, name='update', out_shape=(shape,) * 8, in_s...  2.98 us

profile of v3, /device:TPU:1, one launch (start us, length us, event | category | flops | bytes accessed | tf_op | source)
XLA Modules:
  0.0 70.3 jit_solution(1743909122196944454)
XLA Ops:
  0.6 0.0 copy-start.5
  0.6 0.0 copy-start.4
  0.7 0.0 copy-start.3
  0.7 0.0 copy-start.2
  0.7 0.0 copy-start.1
  0.7 0.0 copy-start
  0.7 66.5 %exchange.1 = (bf16[16,128,512]{2,1,0:T(8,128)(2,1)S(1)}, bf16[16,128,512]{2,1,0:T(8,128)(2,1)S(1)}, f32[8,128]{1,0:T(8,128)S(1)}) custom-call(bf16[2,128,4096]{2,1,0:T(8,128)(2,1)} %first_ref.1, bf16[2,128,4096]{2,1,0:T(8,128)(2,1)} %second_ref.1), custom_call_target="tpu_custom_call" | custom-call | tf_op jit(solution)/shard_map/exchange/pallas_call | solution.py:289
  67.2 0.0 copy-done.5
  67.2 0.0 copy-done.4
  67.2 0.0 copy-done.3
  67.2 0.0 copy-done.2
  67.3 0.0 copy-done.1
  67.3 0.0 copy-done
  67.3 3.0 %update.1 = (f32[128,512]{1,0:T(8,128)}, f32[128,512]{1,0:T(8,128)}, f32[128,512]{1,0:T(8,128)}, f32[128,512]{1,0:T(8,128)}, f32[128,512]{1,0:T(8,128)}, /*index...) custom-call(f32[8,128]{1,0:T(8,128)S(1)} %get-tuple-element.11.gram_ref, ...), custom_call_target="tpu_custom_call" | custom-call | tf_op jit(solution)/shard_map/update/pallas_call | solution.py:315
Async XLA Ops:
  0.6 66.6 %copy-start.5 = (f32[128,512]{1,0:T(8,128)S(1)}, f32[128,512]{1,0:T(8,128)}, u32[]{:S(2)}) copy-start(f32[128,512]{1,0:T(8,128)} %second_v.1) | copy-start | bytes 786436
  0.6 66.6 %copy-start.4 = (f32[128,512]{1,0:T(8,128)S(1)}, f32[128,512]{1,0:T(8,128)}, u32[]{:S(2)}) copy-start(f32[128,512]{1,0:T(8,128)} %second_m.1) | copy-start | bytes 786436
  0.7 66.6 %copy-start.3 = (f32[128,512]{1,0:T(8,128)S(1)}, f32[128,512]{1,0:T(8,128)}, u32[]{:S(2)}) copy-start(f32[128,512]{1,0:T(8,128)} %second_w.1) | copy-start | bytes 786436
  0.7 66.6 %copy-start.2 = (f32[128,512]{1,0:T(8,128)S(1)}, f32[128,512]{1,0:T(8,128)}, u32[]{:S(2)}) copy-start(f32[128,512]{1,0:T(8,128)} %first_v.1) | copy-start | bytes 786436
  0.7 66.6 %copy-start.1 = (f32[128,512]{1,0:T(8,128)S(1)}, f32[128,512]{1,0:T(8,128)}, u32[]{:S(2)}) copy-start(f32[128,512]{1,0:T(8,128)} %first_m.1) | copy-start | bytes 786436
  0.7 66.6 %copy-start = (f32[128,512]{1,0:T(8,128)S(1)}, f32[128,512]{1,0:T(8,128)}, u32[]{:S(2)}) copy-start(f32[128,512]{1,0:T(8,128)} %first_w.1) | copy-start | bytes 786436

commit v4 on v3

--- a/solution.py
+++ b/solution.py
@@ -201,6 +201,24 @@
 
 
 UPDATE_ROWS = 32
+
+
+def spread_weights(mixes, group):
+    size = TASKS * ROW_BLOCK
+    row = lax.broadcasted_iota(jnp.int32, (ROW_BLOCK, size), 0)
+    column = lax.broadcasted_iota(jnp.int32, (ROW_BLOCK, size), 1)
+    lane = group * (LANES // 2)
+    weights = jnp.zeros((ROW_BLOCK, size), jnp.float32)
+    for task in range(TASKS):
+        value = jnp.broadcast_to(mixes[task : task + 1, lane : lane + 1], (ROW_BLOCK, size))
+        weights = jnp.where(column == task * ROW_BLOCK + row, value, weights)
+    parts = []
+    rest = weights
+    for _ in range(3):
+        part = rest.astype(jnp.bfloat16)
+        parts.append(part)
+        rest = rest - part.astype(jnp.float32)
+    return jnp.concatenate(parts, axis=0)
 
 
 def update_kernel(
@@ -238,16 +256,17 @@
     retained = (first_ref, second_ref)
     stores = []
     for group in range(2):
-        lanes = slice(group * (LANES // 2), group * (LANES // 2) + 1)
-        weights_of = [
-            jnp.broadcast_to(mixes[task : task + 1, lanes], (1, width)) for task in range(TASKS)
-        ]
+        weights_of = spread_weights(mixes, group)
         for block in range(rows_all // UPDATE_ROWS):
             rows = slice(block * UPDATE_ROWS, (block + 1) * UPDATE_ROWS)
-            combined = None
-            for task in range(TASKS):
-                term = weights_of[task] * retained[group][task, rows, :].astype(jnp.float32)
-                combined = term if combined is None else combined + term
+            pieces = []
+            for row in range(rows.start, rows.stop, ROW_BLOCK):
+                side = retained[group][:, row : row + ROW_BLOCK, :].reshape(TASKS * ROW_BLOCK, width)
+                product = jnp.dot(weights_of, side, preferred_element_type=jnp.float32)
+                pieces.append(
+                    product[:ROW_BLOCK] + (product[ROW_BLOCK : 2 * ROW_BLOCK] + product[2 * ROW_BLOCK :])
+                )
+            combined = jnp.concatenate(pieces, axis=0)
             weights = stored[group][0][rows, :]
             moment = stored[group][1][rows, :]
             variance = stored[group][2][rows, :]

time: 70.3 us -> 69.9 us (level)
  no operation moved by 1% of the time
where the time goes in v4:
time: 69.9 us
  Pallas kernels  69.1 us (99%)
  between operations  0.74 us (1%)
    pallas_call x1, Pallas kernels, local(): pl.pallas_call(exchange_kernel, name='exchange', out_shape=(pltpu.VMEM((T...  66.5 us
    pallas_call x1, Pallas kernels, local(): pl.pallas_call(update_kernel, name='update', out_shape=(shape,) * 8, in_s...  2.59 us

profile of v4, /device:TPU:1, one launch (start us, length us, event | category | flops | bytes accessed | tf_op | source)
XLA Modules:
  0.0 69.9 jit_solution(10867121174672873341)
XLA Ops:
  0.6 0.0 copy-start.5
  0.6 0.0 copy-start.4
  0.7 0.0 copy-start.3
  0.7 0.0 copy-start.2
  0.7 0.0 copy-start.1
  0.7 0.0 copy-start
  0.7 66.5 %exchange.1 = (bf16[16,128,512]{2,1,0:T(8,128)(2,1)S(1)}, bf16[16,128,512]{2,1,0:T(8,128)(2,1)S(1)}, f32[8,128]{1,0:T(8,128)S(1)}) custom-call(bf16[2,128,4096]{2,1,0:T(8,128)(2,1)} %first_ref.1, bf16[2,128,4096]{2,1,0:T(8,128)(2,1)} %second_ref.1), custom_call_target="tpu_custom_call" | custom-call | tf_op jit(solution)/shard_map/exchange/pallas_call | solution.py:308
  67.2 0.0 copy-done.5
  67.2 0.0 copy-done.4
  67.2 0.0 copy-done.3
  67.2 0.0 copy-done.2
  67.3 0.0 copy-done.1
  67.3 0.0 copy-done
  67.3 2.6 %update.1 = (f32[128,512]{1,0:T(8,128)}, f32[128,512]{1,0:T(8,128)}, f32[128,512]{1,0:T(8,128)}, f32[128,512]{1,0:T(8,128)}, f32[128,512]{1,0:T(8,128)}, /*index...) custom-call(f32[8,128]{1,0:T(8,128)S(1)} %get-tuple-element.11.gram_ref, ...), custom_call_target="tpu_custom_call" | custom-call | tf_op jit(solution)/shard_map/update/pallas_call | solution.py:334
Async XLA Ops:
  0.6 66.6 %copy-start.5 = (f32[128,512]{1,0:T(8,128)S(1)}, f32[128,512]{1,0:T(8,128)}, u32[]{:S(2)}) copy-start(f32[128,512]{1,0:T(8,128)} %second_v.1) | copy-start | bytes 786436
  0.6 66.6 %copy-start.4 = (f32[128,512]{1,0:T(8,128)S(1)}, f32[128,512]{1,0:T(8,128)}, u32[]{:S(2)}) copy-start(f32[128,512]{1,0:T(8,128)} %second_m.1) | copy-start | bytes 786436
  0.7 66.6 %copy-start.3 = (f32[128,512]{1,0:T(8,128)S(1)}, f32[128,512]{1,0:T(8,128)}, u32[]{:S(2)}) copy-start(f32[128,512]{1,0:T(8,128)} %second_w.1) | copy-start | bytes 786436
  0.7 66.6 %copy-start.2 = (f32[128,512]{1,0:T(8,128)S(1)}, f32[128,512]{1,0:T(8,128)}, u32[]{:S(2)}) copy-start(f32[128,512]{1,0:T(8,128)} %first_v.1) | copy-start | bytes 786436
  0.7 66.6 %copy-start.1 = (f32[128,512]{1,0:T(8,128)S(1)}, f32[128,512]{1,0:T(8,128)}, u32[]{:S(2)}) copy-start(f32[128,512]{1,0:T(8,128)} %first_m.1) | copy-start | bytes 786436
  0.7 66.6 %copy-start = (f32[128,512]{1,0:T(8,128)S(1)}, f32[128,512]{1,0:T(8,128)}, u32[]{:S(2)}) copy-start(f32[128,512]{1,0:T(8,128)} %first_w.1) | copy-start | bytes 786436
